TPU v7x, 32 devices: a whole 2x2x4 slice. The times are simulated.
32 devices in a mesh: col: 4 (over y, x), tile: 8 (over z, core).
Axes of the slice: x: 2, y: 2, z: 4, core: 2. Of those that a mesh axis runs over, the one named last changes fastest.
Arguments:
- vectors: float32 [8, 4, 64, 2048], P(None, None, 'tile', 'col'), may hold values from -12 to 12
- onsite: float32 [4, 64, 2048], P(None, 'tile', 'col'), may hold values from -0.3 to 0.3
- intra_hop: float32 [3, 2, 64, 2048], P(None, None, 'tile', 'col'), may hold values from 0.15 to 0.35
- inter_index: int32 [4, 2, 64, 2048], P(None, None, 'tile', 'col'), may hold values from 0 to 18
- inter_hop: float32 [4, 2, 64, 2048], P(None, None, 'tile', 'col'), may hold values from 0.04 to 0.16
Outputs:
- last_term: float32 [8, 4, 64, 2048], P(None, None, 'tile', 'col')
- moments: float32 [7, 8], replicated
Inputs may be any that keep to these rules, and one draw needn't show every extreme that they name: `inter_index`: A code c below 18 names the second-layer orbital of sublattice c // 9 in the cell at offset ((c % 9) // 3 - 1, c % 3 - 1) from the slot's cell; 18 marks an empty slot.
All inputs are finite; a program needn't handle non-finite values.
Results may differ from a plain program's by a relative error of at most 0.000025.
Values sent between devices are 32-bit elements; how exact they have to be, the bound alone decides.
A program may use at most 64 MiB of HBM per device.

v0:
```python
import jax
import jax.numpy as jnp
from jax import lax
from jax.sharding import PartitionSpec as P

BOND_OFFSETS = ((0, 0), (-1, 0), (0, -1))


def extended_2(cells, sides, width):
    for axis, dim in sides:
        count = lax.axis_size(axis)
        head = lax.slice_in_dim(cells, 0, width, axis=dim)
        tail = lax.slice_in_dim(cells, cells.shape[dim] - width, cells.shape[dim], axis=dim)
        cells = jnp.concatenate(
            [
                lax.ppermute(tail, axis, [(i, (i + 1) % count) for i in range(count)]),
                cells,
                lax.ppermute(head, axis, [((i + 1) % count, i) for i in range(count)]),
            ],
            axis=dim,
        )
    return cells


def sliced(array, row_off, col_off):
    rows = array.shape[-2] - 2
    cols = array.shape[-1] - 2
    return array[..., 1 + row_off : 1 + row_off + rows, 1 + col_off : 1 + col_off + cols]


def trim_rim(array, excess):
    return array[..., excess : array.shape[-2] - excess, excess : array.shape[-1] - excess]


def make_weights(neighbours, amplitude):
    return jnp.stack(
        [
            jnp.sum(jnp.where(neighbours == code_no, amplitude, jnp.zeros_like(amplitude)), axis=0)
            for code_no in range(18)
        ],
        axis=1,
    )


def apply_hamiltonian(vector, onsite, intra_hop, weights, pick):
    outputs = []
    for layer_no in range(2):
        side_a = vector[:, 2 * layer_no]
        side_b = vector[:, 2 * layer_no + 1]
        out_a = pick(onsite[2 * layer_no], 0, 0) * pick(side_a, 0, 0)
        out_b = pick(onsite[2 * layer_no + 1], 0, 0) * pick(side_b, 0, 0)
        for bond_idx in range(3):
            row_off, col_off = BOND_OFFSETS[bond_idx]
            out_a = out_a + pick(intra_hop[bond_idx, layer_no], 0, 0) * pick(
                side_b, row_off, col_off
            )
            out_b = out_b + pick(intra_hop[bond_idx, layer_no], -row_off, -col_off) * pick(
                side_a, -row_off, -col_off
            )
        outputs += [out_a, out_b]
    for source in range(2):
        for code_no in range(18):
            target = code_no // 9
            row_off = code_no % 9 // 3 - 1
            col_off = code_no % 3 - 1
            outputs[source] = outputs[source] + pick(weights[source, code_no], 0, 0) * pick(
                vector[:, 2 + target], row_off, col_off
            )
            outputs[2 + target] = outputs[2 + target] + pick(
                weights[source, code_no], -row_off, -col_off
            ) * pick(vector[:, source], -row_off, -col_off)
    return jnp.stack(outputs, axis=1)


def inner_sums(left, right):
    return jnp.sum(left * right, axis=(1, 2, 3))


def moments_from(totals, orbitals):
    scaled = totals / orbitals
    zeroth = scaled[0]
    first = scaled[1]
    return jnp.stack(
        [
            zeroth,
            first,
            2.0 * scaled[2] - zeroth,
            2.0 * scaled[3] - first,
            2.0 * scaled[4] - zeroth,
            2.0 * scaled[5] - first,
            2.0 * scaled[6] - zeroth,
        ]
    )


def reduce_group(group):
    return lax.psum(group, ("col", "tile"))


def on_device(vectors, onsite, intra_hop, inter_index, inter_hop):
    slots = inter_index.shape[0]
    rows = vectors.shape[2]
    cols = vectors.shape[3]
    rim_width = 3
    packed = jnp.concatenate(
        [onsite, intra_hop.reshape(6, rows, cols), inter_hop.reshape(2 * slots, rows, cols)], axis=0
    )
    packed = extended_2(packed, (("col", 2), ("tile", 1)), rim_width)
    codes = extended_2(
        inter_index.reshape(2 * slots, rows, cols), (("col", 2), ("tile", 1)), rim_width
    )
    wide_rows = packed.shape[1]
    wide_cols = packed.shape[2]
    weights = make_weights(
        codes.reshape(slots, 2, wide_rows, wide_cols),
        packed[10:].reshape(slots, 2, wide_rows, wide_cols),
    )

    def operator(extended, margin):
        excess = rim_width - margin
        local_coef = trim_rim(packed, excess)
        return apply_hamiltonian(
            extended,
            local_coef[:4],
            local_coef[4:10].reshape(3, 2, local_coef.shape[1], local_coef.shape[2]),
            trim_rim(weights, excess),
            sliced,
        )

    wide_zero = extended_2(vectors, (("col", 3), ("tile", 2)), 3)
    wide_one = operator(wide_zero, 3)
    wide_two = 2.0 * operator(wide_one, 2) - trim_rim(wide_zero, 2)
    last_term = 2.0 * operator(wide_two, 1) - trim_rim(wide_one, 2)
    term_one = trim_rim(wide_one, 2)
    term_two = trim_rim(wide_two, 1)
    orbitals = 4 * rows * cols * lax.axis_size("tile") * lax.axis_size("col")
    first_group = reduce_group(
        jnp.stack(
            [
                inner_sums(vectors, vectors),
                inner_sums(term_one, vectors),
                inner_sums(term_one, term_one),
            ]
        )
    )
    second_group = reduce_group(
        jnp.stack([inner_sums(term_two, term_one), inner_sums(term_two, term_two)])
    )
    third_group = reduce_group(
        jnp.stack([inner_sums(last_term, term_two), inner_sums(last_term, last_term)])
    )
    totals = jnp.concatenate([first_group, second_group, third_group], axis=0)
    return (last_term, moments_from(totals, orbitals))


def solution(mesh):
    placed = (
        P(None, None, "tile", "col"),
        P(None, "tile", "col"),
        P(None, None, "tile", "col"),
        P(None, None, "tile", "col"),
        P(None, None, "tile", "col"),
    )
    return jax.shard_map(
        on_device,
        mesh=mesh,
        in_specs=placed,
        out_specs=(P(None, None, "tile", "col"), P()),
        check_vma=False,
    )
```

profile of v0, /device:TPU:0, one launch (start us, length us, event | category | flops | bytes accessed | tf_op | source)
XLA Modules:
  0.0 132.9 jit_solution(14603102076972150795)
XLA Ops:
  0.7 1.1 fusion.1
  1.8 4.0 %collective-permute-start.5 = (f32[8,4,8,3]{3,2,0,1:T(8,128)S(1)}, f32[8,4,8,3]{3,2,0,1:T(8,128)S(1)}, u32[]{:S(2)}, u32[]{:S(2)}) collective-permute-start(f32[8,4,8,3]{3,2,0,1:T(8,128)S(1)} %get-tuple-element.54), channel_id=1, source_target_pairs={{8,0},{16,8},{24,16},{0,24},{9,1},{17,9},{25,17},{1,25},{10,2},{18... | collective-permute-start | bytes 9224 | tf_op jit(solution)/shard_map/ppermute | solution.py:18
  5.8 0.8 fusion.4
  6.6 2.9 %collective-permute-start.9 = (s32[8,8,3]{2,1,0:T(8,128)S(1)}, s32[8,8,3]{2,1,0:T(8,128)S(1)}, u32[]{:S(2)}, u32[]{:S(2)}) collective-permute-start(s32[8,8,3]{2,1,0:T(8,128)S(1)} %get-tuple-element.80), channel_id=1, source_target_pairs={{8,0},{16,8},{24,16},{0,24},{9,1},{17,9},{25,17},{1,25},{10,2},{18... | collective-permute-start | bytes 2312 | tf_op jit(solution)/shard_map/ppermute | solution.py:18
  9.5 0.9 pad_maximum_fusion.9
  10.5 3.0 %collective-permute-start.1 = (f32[18,8,3]{2,1,0:T(8,128)S(1)}, f32[18,8,3]{2,1,0:T(8,128)S(1)}, u32[]{:S(2)}, u32[]{:S(2)}) collective-permute-start(f32[18,8,3]{2,1,0:T(8,128)S(1)} %get-tuple-element.58), channel_id=1, source_target_pairs={{8,0},{16,8},{24,16},{0,24},{9,1},{17,9},{25,17},{1,25},{10,2},{18... | collective-permute-start | bytes 5192 | tf_op jit(solution)/shard_map/ppermute | solution.py:18
  13.5 1.4 %collective-permute-start = (f32[18,8,3]{2,1,0:T(8,128)S(1)}, f32[18,8,3]{2,1,0:T(8,128)S(1)}, u32[]{:S(2)}, u32[]{:S(2)}) collective-permute-start(f32[18,8,3]{2,1,0:T(8,128)S(1)} %get-tuple-element.57), channel_id=1, source_target_pairs={{0,8},{8,16},{16,24},{24,0},{1,9},{9,17},{17,25},{25,1},{2,10},{10... | collective-permute-start | bytes 5192 | tf_op jit(solution)/shard_map/ppermute | solution.py:16
  14.9 1.0 pad_add_fusion.1
  16.0 1.5 %collective-permute-start.11 = (s32[8,3,518]{2,1,0:T(4,128)S(1)}, s32[8,3,518]{2,1,0:T(4,128)S(1)}, u32[]{:S(2)}, u32[]{:S(2)}) collective-permute-start(s32[8,3,518]{2,1,0:T(4,128)S(1)} %get-tuple-element.78), channel_id=1, source_target_pairs={{1,0},{2,1},{3,2},{4,3},{5,4},{6,5},{7,6},{0,7},{9,8},{10,9},{11,1... | collective-permute-start | bytes 149192 | tf_op jit(solution)/shard_map/ppermute | solution.py:18
  17.4 1.3 collective-permute-done
  19.0 2.3 %collective-permute-start.3 = (f32[18,3,518]{2,1,0:T(4,128)S(1)}, f32[18,3,518]{2,1,0:T(4,128)S(1)}, u32[]{:S(2)}, u32[]{:S(2)}) collective-permute-start(f32[18,3,518]{2,1,0:T(4,128)S(1)} %get-tuple-element.56), channel_id=1, source_target_pairs={{1,0},{2,1},{3,2},{4,3},{5,4},{6,5},{7,6},{0,7},{9,8},{10,9},{11,1... | collective-permute-start | bytes 335672 | tf_op jit(solution)/shard_map/ppermute | solution.py:18
  22.3 0.9 fusion
  23.2 3.5 %collective-permute-start.7 = (f32[8,4,3,518]{3,2,0,1:T(4,128)}, f32[8,4,3,518]{3,2,0,1:T(4,128)}, u32[]{:S(2)}, u32[]{:S(2)}) collective-permute-start(f32[8,4,3,518]{3,2,0,1:T(4,128)} %get-tuple-element.52), channel_id=1, source_target_pairs={{1,0},{2,1},{3,2},{4,3},{5,4},{6,5},{7,6},{0,7},{9,8},{10,9},{11,1... | collective-permute-start | bytes 596744 | tf_op jit(solution)/shard_map/ppermute | solution.py:18
  26.7 1.5 %collective-permute-done.2 = f32[18,3,518]{2,1,0:T(4,128)S(1)} collective-permute-done((f32[18,3,518]{2,1,0:T(4,128)S(1)}, f32[18,3,518]{2,1,0:T(4,128)S(1)}, u32[]{:S(2)}, u32[]{:S(2)}) %collective-permute-start.2) | collective-permute-done | bytes 111920 | tf_op jit(solution)/shard_map/ppermute | solution.py:16
  28.6 1.0 slice.2840
  31.1 0.7 slice_bitcast_fusion.29
  34.6 0.7 slice_bitcast_fusion.73
  36.9 0.7 slice_bitcast_fusion.74
  37.6 0.7 slice_bitcast_fusion.32
  41.8 0.7 slice_bitcast_fusion.35
  44.1 0.7 slice_bitcast_fusion.36
  47.0 0.8 slice.3097
  48.5 0.7 slice_bitcast_fusion.75
  49.2 0.7 slice_bitcast_fusion.33
  50.8 0.7 slice_bitcast_fusion.80
  52.9 0.7 slice_bitcast_fusion.81
  53.6 0.7 slice_bitcast_fusion.39
  55.0 0.7 slice_bitcast_fusion.82
  55.7 0.7 slice_bitcast_fusion.40
  57.3 0.7 slice_bitcast_fusion.83
  60.3 0.9 compare_select_fusion.13
  61.2 1.0 reduce_sum.227
  62.3 0.7 slice_bitcast_fusion.44
  63.2 0.7 slice_bitcast_fusion.45
  64.0 0.7 slice_bitcast_fusion.46
  67.7 0.9 slice.3196
  68.6 0.9 slice.3150
  77.0 1.6 %pad_maximum_fusion = f32[8,4,14,518]{3,2,0,1:T(8,128)S(1)} fusion(f32[8,4,3,518]{3,2,0,1:T(4,128)} %collective-permute-done.7, f32[8,4,8,3]{3,2,0,1:T(8,128)S(1)} %copy-done.9, f32[8,4,8,3]{3,2,0,1:T(8,128)S(1)} %copy-done.11, f32[8,4,3,518]{3,2,0,1:T(4,128)} %collective-permute-done.6, f32[8,4,8,512]{3,2,1,0:T(8,128)S(1)} %copy-done.4), kind=kLoop, calls=%fused_computation.1 | loop fusion | flops 928256 | bytes 1856512 | tf_op jit(solution)/shard_map/concatenate | solution.py:14
  78.8 1.5 %multiply_add_fusion = f32[8,12,516]{2,1,0:T(8,128)S(1)} fusion(f32[8,14,518]{2,1,0:T(8,128)S(1)} %get-tuple-element.19, f32[8,14,518]{2,1,0:T(8,128)S(1)} %get-tuple-element.20, f32[8,14,518]{2,1,0:T(8,128)S(1)} %get-tuple-element.18, f32[8,14,518]{2,1,0:T(8,128)S(1)} %get-tuple-element.17, f32[12,516]{1,0:T(8,128)S(1)} %get-tuple-element.410, ...), kind=kLoop, calls=%fused_computation.31 | loop fusion | flops 2130048 | bytes 5102208 | tf_op jit(solution)/shard_map/add | solution.py:69
  80.2 1.6 %multiply_add_fusion.1 = f32[8,12,516]{2,1,0:T(8,128)S(1)} fusion(f32[8,14,518]{2,1,0:T(8,128)S(1)} %get-tuple-element.19, f32[8,14,518]{2,1,0:T(8,128)S(1)} %get-tuple-element.20, f32[8,14,518]{2,1,0:T(8,128)S(1)} %get-tuple-element.17, f32[8,14,518]{2,1,0:T(8,128)S(1)} %get-tuple-element.18, f32[12,516]{1,0:T(8,128)S(1)} %get-tuple-element.426, ...), kind=kLoop, calls=%fused_computation.32 | loop fusion | flops 2130048 | bytes 5102208 | tf_op jit(solution)/shard_map/add | solution.py:69
  81.8 1.4 %multiply_add_fusion.2 = f32[8,12,516]{2,1,0:T(8,128)S(1)} fusion(f32[8,14,518]{2,1,0:T(8,128)S(1)} %get-tuple-element.17, f32[8,14,518]{2,1,0:T(8,128)S(1)} %get-tuple-element.18, f32[8,14,518]{2,1,0:T(8,128)S(1)} %get-tuple-element.20, f32[8,14,518]{2,1,0:T(8,128)S(1)} %get-tuple-element.19, f32[12,516]{1,0:T(8,128)S(1)} %get-tuple-element.411, ...), kind=kLoop, calls=%fused_computation.33 | loop fusion | flops 2130048 | bytes 5102208 | tf_op jit(solution)/shard_map/add | solution.py:66
  83.2 1.4 %multiply_add_fusion.3 = f32[8,12,516]{2,1,0:T(8,128)S(1)} fusion(f32[8,14,518]{2,1,0:T(8,128)S(1)} %get-tuple-element.17, f32[8,14,518]{2,1,0:T(8,128)S(1)} %get-tuple-element.18, f32[8,14,518]{2,1,0:T(8,128)S(1)} %get-tuple-element.19, f32[8,14,518]{2,1,0:T(8,128)S(1)} %get-tuple-element.20, f32[12,516]{1,0:T(8,128)S(1)} %get-tuple-element.367, ...), kind=kLoop, calls=%fused_computation.34 | loop fusion | flops 2130048 | bytes 5102208 | tf_op jit(solution)/shard_map/add | solution.py:66
  84.6 1.5 %add_bitcast_fusion = f32[8,1,10,514]{3,2,0,1:T(8,128)S(1)} fusion(f32[8,12,516]{2,1,0:T(8,128)S(1)} %multiply_add_fusion.2, f32[8,12,516]{2,1,0:T(8,128)S(1)} %multiply_add_fusion.3, f32[8,12,516]{2,1,0:T(8,128)S(1)} %multiply_add_fusion.1, f32[8,12,516]{2,1,0:T(8,128)S(1)} %multiply_add_fusion, f32[10,514]{1,0:T(8,128)S(1)} %get-tuple-element.446, ...), kind=kLoop, calls=%fused_computation.27 | loop fusion | flops 1768160 | bytes 4235360 | tf_op jit(solution)/shard_map/stack | solution.py:72
  86.1 1.4 %add_bitcast_fusion.1 = f32[8,1,10,514]{3,2,0,1:T(8,128)S(1)} fusion(f32[8,12,516]{2,1,0:T(8,128)S(1)} %multiply_add_fusion.2, f32[8,12,516]{2,1,0:T(8,128)S(1)} %multiply_add_fusion.3, f32[8,12,516]{2,1,0:T(8,128)S(1)} %multiply_add_fusion, f32[8,12,516]{2,1,0:T(8,128)S(1)} %multiply_add_fusion.1, f32[10,514]{1,0:T(8,128)S(1)} %get-tuple-element.466, ...), kind=kLoop, calls=%fused_computation.28 | loop fusion | flops 1768160 | bytes 4235360 | tf_op jit(solution)/shard_map/stack | solution.py:72
  87.4 1.5 %add_bitcast_fusion.2 = f32[8,1,10,514]{3,2,0,1:T(8,128)S(1)} fusion(f32[8,12,516]{2,1,0:T(8,128)S(1)} %multiply_add_fusion, f32[8,12,516]{2,1,0:T(8,128)S(1)} %multiply_add_fusion.1, f32[8,12,516]{2,1,0:T(8,128)S(1)} %multiply_add_fusion.3, f32[8,12,516]{2,1,0:T(8,128)S(1)} %multiply_add_fusion.2, f32[10,514]{1,0:T(8,128)S(1)} %get-tuple-element.447, ...), kind=kLoop, calls=%fused_computation.29 | loop fusion | flops 1768160 | bytes 4235360 | tf_op jit(solution)/shard_map/stack | solution.py:72
  88.9 1.4 %add_bitcast_fusion.3 = f32[8,1,10,514]{3,2,0,1:T(8,128)S(1)} fusion(f32[8,12,516]{2,1,0:T(8,128)S(1)} %multiply_add_fusion, f32[8,12,516]{2,1,0:T(8,128)S(1)} %multiply_add_fusion.1, f32[8,12,516]{2,1,0:T(8,128)S(1)} %multiply_add_fusion.2, f32[8,12,516]{2,1,0:T(8,128)S(1)} %multiply_add_fusion.3, f32[10,514]{1,0:T(8,128)S(1)} %get-tuple-element.295, ...), kind=kLoop, calls=%fused_computation.30 | loop fusion | flops 1768160 | bytes 4235360 | tf_op jit(solution)/shard_map/stack | solution.py:72
  93.3 1.4 %multiply_reduce_fusion.6 = (f32[8]{0:T(128)S(1)}, f32[8]{0:T(128)S(1)}, f32[8]{0:T(128)S(1)}, f32[8]{0:T(128)S(1)}, f32[8]{0:T(128)S(1)}, /*index=5*/f32[8]{0:T(128)S(1)}, f32[8]{0:T(128)S(1)}, f32[8,4,8,512]{3,2,1,0:T(8,128)}) fusion(f32[8,4,8,512]{3,2,1,0:T(8,128)S(1)} %copy-done.4, f32[8,1,12,516]{3,2,1,0:T(8,128)S(1)} %bitcast.367, ...), kind=kLoop, calls=%fused_computation.16 | loop fusion | flops 2883528 | bytes 3408096 | tf_op jit(solution)/shard_map/reduce_sum | solution.py:76
  94.7 37.5 %all-reduce = (f32[2,8]{1,0:T(2,128)S(1)}, f32[2,8]{1,0:T(2,128)S(1)}, f32[3,8]{1,0:T(4,128)S(1)}) all-reduce(f32[2,8]{1,0:T(2,128)S(1)} %pad_maximum_fusion.12, f32[2,8]{1,0:T(2,128)S(1)} %pad_maximum_fusion.11, f32[3,8]{1,0:T(4,128)S(1)} %pad_maximum_fusion.10), channel_id=1, replica_groups=mesh['col'=4,'tile'=8] {'col','tile'}, use_global_device_ids=true, to_apply=%region_27.28 | all-reduce | flops 56 | bytes 448 | tf_op jit(solution)/shard_map/psum | solution.py:97
  (380 shorter events, 34.1 us)
Async XLA Ops:
  0.6 18.1 %copy-start.1 = (f32[4,2,8,512]{3,2,1,0:T(8,128)S(1)}, f32[4,2,8,512]{3,2,1,0:T(8,128)}, u32[]{:S(2)}) copy-start(f32[4,2,8,512]{3,2,1,0:T(8,128)} %param.9) | copy-start | bytes 393220
  0.6 18.1 %copy-start.2 = (f32[3,2,8,512]{3,2,1,0:T(8,128)S(1)}, f32[3,2,8,512]{3,2,1,0:T(8,128)}, u32[]{:S(2)}) copy-start(f32[3,2,8,512]{3,2,1,0:T(8,128)} %param.7) | copy-start | bytes 294916
  0.7 18.1 %copy-start.5 = (f32[4,8,512]{2,1,0:T(8,128)S(1)}, f32[4,8,512]{2,1,0:T(8,128)}, u32[]{:S(2)}) copy-start(f32[4,8,512]{2,1,0:T(8,128)} %param.6) | copy-start | bytes 196612
  1.8 19.5 %collective-permute-start.5 = (f32[8,4,8,3]{3,2,0,1:T(8,128)S(1)}, f32[8,4,8,3]{3,2,0,1:T(8,128)S(1)}, u32[]{:S(2)}, u32[]{:S(2)}) collective-permute-start(f32[8,4,8,3]{3,2,0,1:T(8,128)S(1)} %get-tuple-element.54), channel_id=1, source_target_pairs={{8,0},{16,8},{24,16},{0,24},{9,1},{17,9},{25,17},{1,25},{10,2},{18... | collective-permute-start | bytes 9224 | tf_op jit(solution)/shard_map/ppermute | solution.py:18
  5.8 15.6 %collective-permute-start.4 = (f32[8,4,8,3]{3,2,0,1:T(8,128)S(1)}, f32[8,4,8,3]{3,2,0,1:T(8,128)S(1)}, u32[]{:S(2)}, u32[]{:S(2)}) collective-permute-start(f32[8,4,8,3]{3,2,0,1:T(8,128)S(1)} %get-tuple-element.53), channel_id=1, source_target_pairs={{0,8},{8,16},{16,24},{24,0},{1,9},{9,17},{17,25},{25,1},{2,10},{10... | collective-permute-start | bytes 9224 | tf_op jit(solution)/shard_map/ppermute | solution.py:16
  6.6 6.8 %collective-permute-start.9 = (s32[8,8,3]{2,1,0:T(8,128)S(1)}, s32[8,8,3]{2,1,0:T(8,128)S(1)}, u32[]{:S(2)}, u32[]{:S(2)}) collective-permute-start(s32[8,8,3]{2,1,0:T(8,128)S(1)} %get-tuple-element.80), channel_id=1, source_target_pairs={{8,0},{16,8},{24,16},{0,24},{9,1},{17,9},{25,17},{1,25},{10,2},{18... | collective-permute-start | bytes 2312 | tf_op jit(solution)/shard_map/ppermute | solution.py:18
  9.5 5.4 %collective-permute-start.8 = (s32[8,8,3]{2,1,0:T(8,128)S(1)}, s32[8,8,3]{2,1,0:T(8,128)S(1)}, u32[]{:S(2)}, u32[]{:S(2)}) collective-permute-start(s32[8,8,3]{2,1,0:T(8,128)S(1)} %get-tuple-element.79), channel_id=1, source_target_pairs={{0,8},{8,16},{16,24},{24,0},{1,9},{9,17},{17,25},{25,1},{2,10},{10... | collective-permute-start | bytes 2312 | tf_op jit(solution)/shard_map/ppermute | solution.py:16
  9.5 12.5 %copy-start.4 = (f32[8,4,8,512]{3,2,1,0:T(8,128)S(1)}, f32[8,4,8,512]{3,2,1,0:T(8,128)}, u32[]{:S(2)}) copy-start(f32[8,4,8,512]{3,2,1,0:T(8,128)} %param.5) | copy-start | bytes 1572868
  10.5 7.0 %collective-permute-start.1 = (f32[18,8,3]{2,1,0:T(8,128)S(1)}, f32[18,8,3]{2,1,0:T(8,128)S(1)}, u32[]{:S(2)}, u32[]{:S(2)}) collective-permute-start(f32[18,8,3]{2,1,0:T(8,128)S(1)} %get-tuple-element.58), channel_id=1, source_target_pairs={{8,0},{16,8},{24,16},{0,24},{9,1},{17,9},{25,17},{1,25},{10,2},{18... | collective-permute-start | bytes 5192 | tf_op jit(solution)/shard_map/ppermute | solution.py:18
  13.5 5.3 %collective-permute-start = (f32[18,8,3]{2,1,0:T(8,128)S(1)}, f32[18,8,3]{2,1,0:T(8,128)S(1)}, u32[]{:S(2)}, u32[]{:S(2)}) collective-permute-start(f32[18,8,3]{2,1,0:T(8,128)S(1)} %get-tuple-element.57), channel_id=1, source_target_pairs={{0,8},{8,16},{16,24},{24,0},{1,9},{9,17},{17,25},{25,1},{2,10},{10... | collective-permute-start | bytes 5192 | tf_op jit(solution)/shard_map/ppermute | solution.py:16
  16.0 13.6 %collective-permute-start.11 = (s32[8,3,518]{2,1,0:T(4,128)S(1)}, s32[8,3,518]{2,1,0:T(4,128)S(1)}, u32[]{:S(2)}, u32[]{:S(2)}) collective-permute-start(s32[8,3,518]{2,1,0:T(4,128)S(1)} %get-tuple-element.78), channel_id=1, source_target_pairs={{1,0},{2,1},{3,2},{4,3},{5,4},{6,5},{7,6},{0,7},{9,8},{10,9},{11,1... | collective-permute-start | bytes 149192 | tf_op jit(solution)/shard_map/ppermute | solution.py:18
  17.4 12.1 %collective-permute-start.10 = (s32[8,3,518]{2,1,0:T(4,128)S(1)}, s32[8,3,518]{2,1,0:T(4,128)S(1)}, u32[]{:S(2)}, u32[]{:S(2)}) collective-permute-start(s32[8,3,518]{2,1,0:T(4,128)S(1)} %get-tuple-element.77), channel_id=1, source_target_pairs={{0,1},{1,2},{2,3},{3,4},{4,5},{5,6},{6,7},{7,0},{8,9},{9,10},{10,1... | collective-permute-start | bytes 149192 | tf_op jit(solution)/shard_map/ppermute | solution.py:16
  19.0 7.8 %collective-permute-start.3 = (f32[18,3,518]{2,1,0:T(4,128)S(1)}, f32[18,3,518]{2,1,0:T(4,128)S(1)}, u32[]{:S(2)}, u32[]{:S(2)}) collective-permute-start(f32[18,3,518]{2,1,0:T(4,128)S(1)} %get-tuple-element.56), channel_id=1, source_target_pairs={{1,0},{2,1},{3,2},{4,3},{5,4},{6,5},{7,6},{0,7},{9,8},{10,9},{11,1... | collective-permute-start | bytes 335672 | tf_op jit(solution)/shard_map/ppermute | solution.py:18
  21.3 6.9 %collective-permute-start.2 = (f32[18,3,518]{2,1,0:T(4,128)S(1)}, f32[18,3,518]{2,1,0:T(4,128)S(1)}, u32[]{:S(2)}, u32[]{:S(2)}) collective-permute-start(f32[18,3,518]{2,1,0:T(4,128)S(1)} %get-tuple-element.55), channel_id=1, source_target_pairs={{0,1},{1,2},{2,3},{3,4},{4,5},{5,6},{6,7},{7,0},{8,9},{9,10},{10,1... | collective-permute-start | bytes 335672 | tf_op jit(solution)/shard_map/ppermute | solution.py:16
  23.2 6.3 %copy-start.3 = (s32[4,2,8,512]{3,2,1,0:T(8,128)S(1)}, s32[4,2,8,512]{3,2,1,0:T(8,128)}, u32[]{:S(2)}) copy-start(s32[4,2,8,512]{3,2,1,0:T(8,128)} %param.8) | copy-start | bytes 393220
  23.2 53.8 %collective-permute-start.7 = (f32[8,4,3,518]{3,2,0,1:T(4,128)}, f32[8,4,3,518]{3,2,0,1:T(4,128)}, u32[]{:S(2)}, u32[]{:S(2)}) collective-permute-start(f32[8,4,3,518]{3,2,0,1:T(4,128)} %get-tuple-element.52), channel_id=1, source_target_pairs={{1,0},{2,1},{3,2},{4,3},{5,4},{6,5},{7,6},{0,7},{9,8},{10,9},{11,1... | collective-permute-start | bytes 596744 | tf_op jit(solution)/shard_map/ppermute | solution.py:18
  26.7 50.3 %collective-permute-start.6 = (f32[8,4,3,518]{3,2,0,1:T(4,128)}, f32[8,4,3,518]{3,2,0,1:T(4,128)}, u32[]{:S(2)}, u32[]{:S(2)}) collective-permute-start(f32[8,4,3,518]{3,2,0,1:T(4,128)} %get-tuple-element.51), channel_id=1, source_target_pairs={{0,1},{1,2},{2,3},{3,4},{4,5},{5,6},{6,7},{7,0},{8,9},{9,10},{10,1... | collective-permute-start | bytes 596744 | tf_op jit(solution)/shard_map/ppermute | solution.py:16
  28.6 31.7 %copy-start = (f32[18,14,518]{2,1,0:T(8,128)}, f32[18,14,518]{2,1,0:T(8,128)S(1)}, u32[]{:S(2)}) copy-start(f32[18,14,518]{2,1,0:T(8,128)S(1)} %pad_maximum_fusion.1) | copy-start | bytes 1566436
  63.0 2.0 %slice-start = ((f32[18,14,518]{2,1,0:T(8,128)}), f32[6,14,518]{2,1,0:T(8,128)S(1)}, s32[]{:S(2)}) async-start(f32[18,14,518]{2,1,0:T(8,128)} %copy-done), calls=%async_computation | async-start | bytes 491520 | tf_op jit(solution)/shard_map/slice | solution.py:125
  67.3 2.7 %copy-start.35 = (f32[14,518]{1,0:T(8,128)S(1)}, f32[14,518]{1,0:T(8,128)}, u32[]{:S(2)}) copy-start(f32[14,518]{1,0:T(8,128)} %get-tuple-element.187) | copy-start | bytes 87028
  67.3 2.7 %copy-start.36 = (f32[14,518]{1,0:T(8,128)S(1)}, f32[14,518]{1,0:T(8,128)}, u32[]{:S(2)}) copy-start(f32[14,518]{1,0:T(8,128)} %get-tuple-element.188) | copy-start | bytes 87028
  67.4 2.8 %copy-start.37 = (f32[14,518]{1,0:T(8,128)S(1)}, f32[14,518]{1,0:T(8,128)}, u32[]{:S(2)}) copy-start(f32[14,518]{1,0:T(8,128)} %get-tuple-element.185) | copy-start | bytes 87028
  67.4 2.8 %copy-start.38 = (f32[14,518]{1,0:T(8,128)S(1)}, f32[14,518]{1,0:T(8,128)}, u32[]{:S(2)}) copy-start(f32[14,518]{1,0:T(8,128)} %get-tuple-element.186) | copy-start | bytes 87028
  67.4 2.9 %copy-start.39 = (f32[14,518]{1,0:T(8,128)S(1)}, f32[14,518]{1,0:T(8,128)}, u32[]{:S(2)}) copy-start(f32[14,518]{1,0:T(8,128)} %get-tuple-element.183) | copy-start | bytes 87028
  67.4 2.9 %copy-start.40 = (f32[14,518]{1,0:T(8,128)S(1)}, f32[14,518]{1,0:T(8,128)}, u32[]{:S(2)}) copy-start(f32[14,518]{1,0:T(8,128)} %get-tuple-element.184) | copy-start | bytes 87028
  67.5 2.9 %copy-start.41 = (f32[14,518]{1,0:T(8,128)S(1)}, f32[14,518]{1,0:T(8,128)}, u32[]{:S(2)}) copy-start(f32[14,518]{1,0:T(8,128)} %get-tuple-element.181) | copy-start | bytes 87028
  67.5 2.9 %copy-start.42 = (f32[14,518]{1,0:T(8,128)S(1)}, f32[14,518]{1,0:T(8,128)}, u32[]{:S(2)}) copy-start(f32[14,518]{1,0:T(8,128)} %get-tuple-element.182) | copy-start | bytes 87028
  67.5 3.0 %copy-start.43 = (f32[14,518]{1,0:T(8,128)S(1)}, f32[14,518]{1,0:T(8,128)}, u32[]{:S(2)}) copy-start(f32[14,518]{1,0:T(8,128)} %get-tuple-element.179) | copy-start | bytes 87028
  67.5 3.0 %copy-start.44 = (f32[14,518]{1,0:T(8,128)S(1)}, f32[14,518]{1,0:T(8,128)}, u32[]{:S(2)}) copy-start(f32[14,518]{1,0:T(8,128)} %get-tuple-element.180) | copy-start | bytes 87028
  74.4 1.5 %copy-start.79 = (f32[10,514]{1,0:T(8,128)S(1)}, f32[10,514]{1,0:T(8,128)}, u32[]{:S(2)}) copy-start(f32[10,514]{1,0:T(8,128)} %get-tuple-element.101) | copy-start | bytes 61684
  74.5 1.6 %copy-start.81 = (f32[10,514]{1,0:T(8,128)S(1)}, f32[10,514]{1,0:T(8,128)}, u32[]{:S(2)}) copy-start(f32[10,514]{1,0:T(8,128)} %get-tuple-element.97) | copy-start | bytes 61684
  74.5 1.6 %copy-start.82 = (f32[10,514]{1,0:T(8,128)S(1)}, f32[10,514]{1,0:T(8,128)}, u32[]{:S(2)}) copy-start(f32[10,514]{1,0:T(8,128)} %get-tuple-element.98) | copy-start | bytes 61684
  74.6 1.6 %copy-start.83 = (f32[10,514]{1,0:T(8,128)S(1)}, f32[10,514]{1,0:T(8,128)}, u32[]{:S(2)}) copy-start(f32[10,514]{1,0:T(8,128)} %get-tuple-element.95) | copy-start | bytes 61684
  74.6 1.6 %copy-start.84 = (f32[10,514]{1,0:T(8,128)S(1)}, f32[10,514]{1,0:T(8,128)}, u32[]{:S(2)}) copy-start(f32[10,514]{1,0:T(8,128)} %get-tuple-element.96) | copy-start | bytes 61684
  74.7 1.6 %copy-start.85 = (f32[10,514]{1,0:T(8,128)S(1)}, f32[10,514]{1,0:T(8,128)}, u32[]{:S(2)}) copy-start(f32[10,514]{1,0:T(8,128)} %get-tuple-element.93) | copy-start | bytes 61684
  74.7 1.6 %copy-start.86 = (f32[10,514]{1,0:T(8,128)S(1)}, f32[10,514]{1,0:T(8,128)}, u32[]{:S(2)}) copy-start(f32[10,514]{1,0:T(8,128)} %get-tuple-element.94) | copy-start | bytes 61684
  74.7 1.7 %copy-start.87 = (f32[10,514]{1,0:T(8,128)S(1)}, f32[10,514]{1,0:T(8,128)}, u32[]{:S(2)}) copy-start(f32[10,514]{1,0:T(8,128)} %get-tuple-element.91) | copy-start | bytes 61684
  74.7 1.7 %copy-start.88 = (f32[10,514]{1,0:T(8,128)S(1)}, f32[10,514]{1,0:T(8,128)}, u32[]{:S(2)}) copy-start(f32[10,514]{1,0:T(8,128)} %get-tuple-element.92) | copy-start | bytes 61684
  74.7 1.8 %copy-start.89 = (f32[10,514]{1,0:T(8,128)S(1)}, f32[10,514]{1,0:T(8,128)}, u32[]{:S(2)}) copy-start(f32[10,514]{1,0:T(8,128)} %get-tuple-element.89) | copy-start | bytes 61684
  74.7 1.8 %copy-start.90 = (f32[10,514]{1,0:T(8,128)S(1)}, f32[10,514]{1,0:T(8,128)}, u32[]{:S(2)}) copy-start(f32[10,514]{1,0:T(8,128)} %get-tuple-element.90) | copy-start | bytes 61684
  74.8 1.8 %copy-start.91 = (f32[10,514]{1,0:T(8,128)S(1)}, f32[10,514]{1,0:T(8,128)}, u32[]{:S(2)}) copy-start(f32[10,514]{1,0:T(8,128)} %get-tuple-element.87) | copy-start | bytes 61684
  74.9 1.8 %copy-start.92 = (f32[10,514]{1,0:T(8,128)S(1)}, f32[10,514]{1,0:T(8,128)}, u32[]{:S(2)}) copy-start(f32[10,514]{1,0:T(8,128)} %get-tuple-element.88) | copy-start | bytes 61684
  74.9 1.8 %copy-start.93 = (f32[10,514]{1,0:T(8,128)S(1)}, f32[10,514]{1,0:T(8,128)}, u32[]{:S(2)}) copy-start(f32[10,514]{1,0:T(8,128)} %get-tuple-element.85) | copy-start | bytes 61684
  74.9 1.8 %copy-start.94 = (f32[10,514]{1,0:T(8,128)S(1)}, f32[10,514]{1,0:T(8,128)}, u32[]{:S(2)}) copy-start(f32[10,514]{1,0:T(8,128)} %get-tuple-element.86) | copy-start | bytes 61684
  75.0 1.8 %copy-start.95 = (f32[10,514]{1,0:T(8,128)S(1)}, f32[10,514]{1,0:T(8,128)}, u32[]{:S(2)}) copy-start(f32[10,514]{1,0:T(8,128)} %get-tuple-element.83) | copy-start | bytes 61684
  75.0 1.8 %copy-start.96 = (f32[10,514]{1,0:T(8,128)S(1)}, f32[10,514]{1,0:T(8,128)}, u32[]{:S(2)}) copy-start(f32[10,514]{1,0:T(8,128)} %get-tuple-element.84) | copy-start | bytes 61684
  75.0 2.0 %copy-start.9 = (f32[8,4,8,3]{3,2,0,1:T(8,128)S(1)}, f32[8,4,8,3]{3,2,0,1:T(8,128)}, u32[]{:S(2)}) copy-start(f32[8,4,8,3]{3,2,0,1:T(8,128)} %copy-done.8) | copy-start | bytes 9220
  75.0 2.0 %copy-start.11 = (f32[8,4,8,3]{3,2,0,1:T(8,128)S(1)}, f32[8,4,8,3]{3,2,0,1:T(8,128)}, u32[]{:S(2)}) copy-start(f32[8,4,8,3]{3,2,0,1:T(8,128)} %copy-done.10) | copy-start | bytes 9220
  (62 other events, 72.7 us)
where the time goes:
time: 134 us; the launch traced here: 133 us
  local copies, waits for them, and re-layouts  47.2 us (35%)
  blocking collectives  37.5 us (28%)
  other arithmetic  24 us (18%)
  starting transfers between devices  18.6 us (14%)
  waiting for transfers between devices  2.79 us (2%)
  between operations  2.79 us (2%)
    psum x1, blocking collectives, reduce_group(): return lax.psum(group, ('col', 'tile'))  37.5 us
    squeeze x54, local copies, waits for them, and re-layouts, apply_hamiltonian(): weights[source, code_no]  31.1 us
    ppermute x6, starting transfers between devices, extended_2(): lax.ppermute(head, axis, [((i + 1) % count, i) for i in range(count)])  17.2 us
    slice x84, local copies, waits for them, and re-layouts, sliced(): array[..., 1 + row_off:1 + row_off + rows, 1 + col_off:1 + col_off + cols]  9.12 us
    another operation x8, other arithmetic, apply_hamiltonian(): return jnp.stack(outputs, axis=1)  8.09 us
    concatenate x5, other arithmetic, extended_2(): jnp.concatenate([lax.ppermute(tail, axis, [(i, (i + 1) % count) for i in...  3.38 us
    add x2, other arithmetic, apply_hamiltonian(): outputs[2 + target]  3.01 us
    slice x5, local copies, waits for them, and re-layouts, extended_2(): lax.slice_in_dim(cells, cells.shape[dim] - width, cells.shape[dim], axis=...  2.98 us
  transfers between devices with their start and end apart: 12, of which 2 were waited for; matrix products, arithmetic and copies ran while one was open for 38% of the time, Pallas kernels for 0%

commit v1 on v0

v1 whole, which is shorter than its diff:
```python
import functools

import jax
import jax.numpy as jnp
from jax import lax
from jax.experimental import pallas as pl
from jax.experimental.pallas import tpu as pltpu
from jax.sharding import PartitionSpec as P

RIM = 3
LANES = 128
CODES = 18
MESH = pl.DeviceIdType.MESH
BONDS = ((0, 0), (-1, 0), (0, -1))
HOP, CODE, SITE, BOND2 = 4, 5, 6, 7


def kernel(
    n_col, n_tile, orbitals,
    v_ref, onsite_ref, intra_ref, index_ref, hop_ref,
    out_ref, mom_ref,
    area, terms, moved, weights, weights_t, bond_t, packs, halo, sums, part, col_buf, col_sum, tile_buf,
    row_send, row_recv, pack_send, pack_recv, col_send, col_recv, tile_send, tile_recv,
):
    rows = v_ref.shape[2]
    cols = v_ref.shape[3]
    blocks = cols // LANES
    ring = cols + LANES
    my_col = lax.axis_index("col")
    my_tile = lax.axis_index("tile")
    lane = lax.broadcasted_iota(jnp.int32, (8, LANES), 1)
    sub = lax.broadcasted_iota(jnp.int32, (8, LANES), 0)

    def col_at(step):
        return lax.rem(my_col + step + n_col, n_col)

    def tile_at(step):
        return lax.rem(my_tile + step + n_tile, n_tile)

    barrier = pltpu.get_barrier_semaphore()
    greeted = [(col_at(c), tile_at(t)) for c in (-1, 1) for t in (-1, 1)]
    greeted += [(col_at(c), my_tile) for c in range(1, n_col)]
    for c, t in greeted:
        pl.semaphore_signal(barrier, inc=1, device_id=(c, t), device_id_type=MESH)

    def greet(i, carry):
        pl.semaphore_signal(barrier, inc=1, device_id=(my_col, lax.rem(my_tile + i, n_tile)), device_id_type=MESH)
        return carry

    lax.fori_loop(1, n_tile, greet, 0)

    own = slice(RIM, RIM + rows)
    for o in range(4):
        area[o, own, :, 0:cols] = jnp.swapaxes(v_ref[:, o], 0, 1)
    area[HOP, own, :, 0:cols] = jnp.swapaxes(hop_ref[...], 0, 1)
    area[CODE, own, :, 0:cols] = jnp.swapaxes(index_ref[...].astype(jnp.float32), 0, 1)
    area[SITE, own, :, 0:cols] = jnp.swapaxes(
        jnp.concatenate([onsite_ref[...], intra_ref[0:4]], axis=0), 0, 1
    )
    area[BOND2, own, :, 0:cols] = jnp.swapaxes(
        jnp.concatenate([intra_ref[4:6], jnp.zeros((6, rows, cols), jnp.float32)], axis=0), 0, 1
    )

    pl.semaphore_wait(barrier, len(greeted) + n_tile - 1)

    row_copies = []
    for way, (src, dst, step) in enumerate(((rows, 0, 1), (RIM, RIM + rows, -1))):
        copy = pltpu.make_async_remote_copy(
            src_ref=area.at[:, src : src + RIM, :, 0:cols],
            dst_ref=area.at[:, dst : dst + RIM, :, 0:cols],
            send_sem=row_send.at[way],
            recv_sem=row_recv.at[way],
            device_id=(my_col, tile_at(step)),
            device_id_type=MESH,
        )
        copy.start()
        row_copies.append(copy)

    def pack(r, carry):
        out = list(carry)
        for g in range(8):
            i = (g % 4) * rows + r
            hit = lane // 4 == i
            left = pltpu.roll(area[g, RIM + r, :, 0:LANES], 4 * i, 1)
            right = pltpu.roll(area[g, RIM + r, :, cols - LANES : cols], lax.rem(4 * i + 4, LANES), 1)
            out[g // 4] = jnp.where(hit, left, out[g // 4])
            out[2 + g // 4] = jnp.where(hit, right, out[2 + g // 4])
        return tuple(out)

    zero = jnp.zeros((8, LANES), jnp.float32)
    packed = lax.fori_loop(0, rows, pack, (zero,) * 4)
    for n in range(4):
        packs[n // 2, n % 2] = packed[n]

    pack_copies = []
    for side, step in ((0, -1), (1, 1)):
        for dt in (0, -1, 1):
            slot = side * 3 + 1 - dt
            copy = pltpu.make_async_remote_copy(
                src_ref=packs.at[side],
                dst_ref=halo.at[slot],
                send_sem=pack_send.at[slot],
                recv_sem=pack_recv.at[slot],
                device_id=(col_at(step), tile_at(dt)),
                device_id_type=MESH,
            )
            copy.start()
            pack_copies.append(copy)

    wide = lax.broadcasted_iota(jnp.int32, (8, ring), 0)

    def rolls(x):
        return pltpu.roll(x, 1, 1), pltpu.roll(x, ring - 1, 1)

    def prepare(r, theirs, dt):
        for g in range(8):
            i = (g % 4) * rows + theirs
            from_right = pltpu.roll(halo[1 + dt, g // 4], lax.rem(LANES - 4 * i, LANES), 1)
            from_left = pltpu.roll(halo[4 + dt, g // 4], LANES - 4 - 4 * i, 1)
            area[g, r, :, cols:ring] = jnp.where(lane < LANES // 2, from_right, from_left)
        for o in range(4):
            moved[0, 0, o, r], moved[0, 1, o, r] = rolls(area[o, r])
        bond_t[r] = rolls(area[BOND2, r])[1]
        for s in range(2):
            for b in range(blocks + 1):
                at = slice(b * LANES, (b + 1) * LANES)
                total = [zero] * 3
                for k in range(4):
                    f = 2 * k + s
                    code = jnp.broadcast_to(area[CODE, r, f : f + 1, at], (8, LANES)).astype(jnp.int32)
                    hop = jnp.broadcast_to(area[HOP, r, f : f + 1, at], (8, LANES))
                    for g in range(3):
                        total[g] = total[g] + jnp.where(code == sub + 8 * g, hop, 0.0)
                for g in range(3):
                    weights[r, s, 8 * g : 8 * g + 8, at] = total[g]
            for g in range(3):
                x = weights[r, s, 8 * g : 8 * g + 8, :]
                back, ahead = rolls(x)
                rest = lax.rem(wide + 8 * g, 3)
                weights_t[r, s, 8 * g : 8 * g + 8, :] = jnp.where(
                    rest == 0, ahead, jnp.where(rest == 2, back, x)
                )

    def term(k, o, r, at):
        return area[o, r, :, at] if k == 0 else terms[k - 1, o, r, :, at]

    def hamiltonian(k, r, at):
        def v(o, row_off, col_off):
            if col_off == 0:
                return term(k, o, r + row_off, at)
            return moved[k, (col_off + 1) // 2, o, r + row_off, :, at]

        def spread(x):
            return jnp.broadcast_to(x, (8, LANES))

        def site(f, row):
            return spread(area[SITE, row, f : f + 1, at])

        outs = []
        for l in range(2):
            a, b = 2 * l, 2 * l + 1
            f0, f1 = site(4 + l, r), site(6 + l, r)
            f2 = spread(area[BOND2, r, l : l + 1, at])
            outs.append(
                site(a, r) * v(a, 0, 0) + f0 * v(b, 0, 0) + f1 * v(b, -1, 0) + f2 * v(b, 0, -1)
            )
            outs.append(
                site(b, r) * v(b, 0, 0)
                + f0 * v(a, 0, 0)
                + site(6 + l, r + 1) * v(a, 1, 0)
                + spread(bond_t[r, l : l + 1, at]) * v(a, 0, 1)
            )
        for s in range(2):
            for c in range(CODES):
                t, e, f = c // 9, c % 9 // 3 - 1, c % 3 - 1
                outs[s] = outs[s] + spread(weights[r, s, c : c + 1, at]) * v(2 + t, e, f)
                outs[2 + t] = outs[2 + t] + spread(weights_t[r - e, s, c : c + 1, at]) * v(s, -e, -f)
        return outs

    def advance(k, r):
        inside = jnp.where((r >= RIM) & (r < RIM + rows), 1.0, 0.0).astype(jnp.float32)
        cross, square, first = zero, zero, zero
        for b in range(blocks + 1 if k < 2 else blocks):
            at = slice(b * LANES, (b + 1) * LANES)
            outs = hamiltonian(k, r, at)
            for o in range(4):
                old = term(k, o, r, at)
                new = outs[o] if k == 0 else 2.0 * outs[o] - term(k - 1, o, r, at)
                terms[k, o, r, :, at] = new
                if b < blocks:
                    cross = cross + new * old
                    square = square + new * new
                    if k == 0:
                        first = first + old * old
        if k == 0:
            sums[0] += inside * first
        sums[2 * k + 1] += inside * cross
        sums[2 * k + 2] += inside * square
        if k < 2:
            for o in range(4):
                moved[k + 1, 0, o, r], moved[k + 1, 1, o, r] = rolls(terms[k, o, r])

    def loop(low, high, body):
        def step(i, carry):
            body(i)
            return carry

        lax.fori_loop(low, high, step, 0)

    for n in range(7):
        sums[n] = zero

    for n in (0, 3):
        pack_copies[n].wait_recv()
    loop(RIM, RIM + rows, lambda r: prepare(r, r - RIM, 0))
    for k in range(3):
        loop(RIM + 1 + k, RIM + rows - 1 - k, functools.partial(advance, k))

    for n in (1, 2, 4, 5):
        pack_copies[n].wait_recv()
    for copy in row_copies:
        copy.wait_recv()
    loop(0, RIM, lambda r: prepare(r, rows - RIM + r, -1))
    loop(0, RIM, lambda r: prepare(RIM + rows + r, r, 1))
    for k in range(3):
        def outer(i, k=k):
            advance(k, k + 1 + i + (i // 3) * (rows - 2 * k - 2))

        loop(0, 6, outer)

    row = jnp.zeros((8, LANES), jnp.float32)
    for n in range(7):
        total = jnp.sum(sums[n], axis=1, keepdims=True)
        row = jnp.where(lane == sub + 8 * n, jnp.broadcast_to(total, (8, LANES)), row)
    part[...] = jnp.sum(row, axis=0, keepdims=True)
    col_buf[my_col] = part[...]
    col_copies = []
    for step in range(1, n_col):
        copy = pltpu.make_async_remote_copy(
            src_ref=part,
            dst_ref=col_buf.at[my_col],
            send_sem=col_send.at[step],
            recv_sem=col_recv.at[step],
            device_id=(col_at(step), my_tile),
            device_id_type=MESH,
        )
        copy.start()
        col_copies.append(copy)
    for o in range(4):
        out_ref[:, o] = jnp.swapaxes(terms[2, o, own, :, 0:cols], 0, 1)

    def col_done(step):
        return pltpu.make_async_remote_copy(
            src_ref=part,
            dst_ref=col_buf.at[col_at(-step)],
            send_sem=col_send.at[step],
            recv_sem=col_recv.at[step],
            device_id=(col_at(step), my_tile),
            device_id_type=MESH,
        )

    for step in range(1, n_col):
        col_done(step).wait_recv()
    total = col_buf[0]
    for n in range(1, n_col):
        total = total + col_buf[n]
    col_sum[...] = total
    tile_buf[my_tile] = col_sum[...]

    def tile_copy(step, slot):
        return pltpu.make_async_remote_copy(
            src_ref=col_sum,
            dst_ref=tile_buf.at[slot],
            send_sem=tile_send.at[step],
            recv_sem=tile_recv.at[step],
            device_id=(my_col, lax.rem(my_tile + step, n_tile)),
            device_id_type=MESH,
        )

    loop(1, n_tile, lambda i: tile_copy(i, my_tile).start())
    for copy in row_copies + pack_copies + col_copies:
        copy.wait_send()
    loop(1, n_tile, lambda i: tile_copy(i, lax.rem(my_tile + n_tile - i, n_tile)).wait_recv())
    loop(1, n_tile, lambda i: tile_copy(i, my_tile).wait_send())
    total = lax.fori_loop(1, n_tile, lambda i, t: t + tile_buf[i], tile_buf[0])
    total = jnp.broadcast_to(total / orbitals, (8, LANES))
    scaled = [pltpu.roll(total, (LANES - 8 * n) % LANES, 1)[0:1, 0:8] for n in range(7)]
    mom_ref[0:1, :] = scaled[0]
    mom_ref[1:2, :] = scaled[1]
    for n in range(2, 7):
        mom_ref[n : n + 1, :] = 2.0 * scaled[n] - scaled[n % 2]


def on_device(n_col, n_tile, vectors, onsite, intra_hop, inter_index, inter_hop):
    count, _, rows, cols = vectors.shape
    slots = inter_index.shape[0]
    assert count == 8 and slots == 4 and rows == 8 and cols % LANES == 0
    tall = rows + 2 * RIM
    ring = cols + LANES
    f32 = jnp.float32
    vmem = pl.BlockSpec(memory_space=pltpu.VMEM)
    dma = pltpu.SemaphoreType.DMA
    return pl.pallas_call(
        functools.partial(kernel, n_col, n_tile, 4 * rows * cols * n_col * n_tile),
        out_shape=(
            jax.ShapeDtypeStruct(vectors.shape, f32),
            jax.ShapeDtypeStruct((7, count), f32),
        ),
        in_specs=[vmem] * 5,
        out_specs=(vmem, vmem),
        scratch_shapes=[
            pltpu.VMEM((8, tall, 8, ring), f32),
            pltpu.VMEM((3, 4, tall, 8, ring), f32),
            pltpu.VMEM((3, 2, 4, tall, 8, ring), f32),
            pltpu.VMEM((tall, 2, 24, ring), f32),
            pltpu.VMEM((tall, 2, 24, ring), f32),
            pltpu.VMEM((tall, 8, ring), f32),
            pltpu.VMEM((2, 2, 8, LANES), f32),
            pltpu.VMEM((6, 2, 8, LANES), f32),
            pltpu.VMEM((7, 8, LANES), f32),
            pltpu.VMEM((1, LANES), f32),
            pltpu.VMEM((n_col, 1, LANES), f32),
            pltpu.VMEM((1, LANES), f32),
            pltpu.VMEM((n_tile, 1, LANES), f32),
            dma((2,)), dma((2,)), dma((6,)), dma((6,)),
            dma((n_col,)), dma((n_col,)), dma((n_tile,)), dma((n_tile,)),
        ],
        compiler_params=pltpu.CompilerParams(
            collective_id=0, has_side_effects=True, vmem_limit_bytes=48 << 20
        ),
    )(
        vectors,
        onsite,
        intra_hop.reshape(6, rows, cols),
        inter_index.reshape(2 * slots, rows, cols),
        inter_hop.reshape(2 * slots, rows, cols),
    )


def solution(mesh):
    spec4, spec3 = P(None, None, "tile", "col"), P(None, "tile", "col")
    return jax.shard_map(
        functools.partial(on_device, mesh.shape["col"], mesh.shape["tile"]),
        mesh=mesh,
        in_specs=(spec4, spec3, spec4, spec4, spec4),
        out_specs=(spec4, P()),
        check_vma=False,
    )
```

time: 134 us -> 35.2 us (0.26)
  local copies, waits for them, and re-layouts: 47.2 us -> 5.96 us
  blocking collectives: 37.5 us -> 0 us
  Pallas kernels: 0 us -> 28.3 us
  other arithmetic: 24 us -> 0 us
  starting transfers between devices: 18.6 us -> 0 us
  waiting for transfers between devices: 2.79 us -> 0 us
  between operations: 2.79 us -> 0.65 us
    psum x1 -> x0, blocking collectives: 37.5 us -> none  [reduce_group(): return lax.psum(group, ('col', 'tile'))]
    squeeze x59 -> x0, local copies, waits for them, and re-layouts: 31.4 us -> none  [the longest x54 31.1 us: apply_hamiltonian(): weights[source, code_no]]
    pallas_call x0 -> x1, Pallas kernels: none -> 28.3 us  [on_device(): pl.pallas_call(functools.partial(kernel, n_col, n_tile, 4 * rows * cols *...]
    ppermute x12 -> x0, starting transfers between devices: 18.6 us -> none  [the longest x6 17.2 us: extended_2(): lax.ppermute(head, axis, [((i + 1) % count, i) for i in range(count)])]
    slice x94 -> x0, local copies, waits for them, and re-layouts: 13.9 us -> none  [the longest x84 9.12 us: sliced(): array[..., 1 + row_off:1 + row_off + rows, 1 + col_off:1 + col_off + cols]]
    another operation x11 -> x0, other arithmetic: 8.12 us -> none  [the longest x8 8.09 us: apply_hamiltonian(): return jnp.stack(outputs, axis=1)]
    add x4 -> x0, other arithmetic: 5.83 us -> none  [the longest x2 3.01 us: apply_hamiltonian(): outputs[2 + target]]
    unnamed x194 -> x12, local copies, waits for them, and re-layouts: 1.25 us -> 5.96 us
  transfers between devices with their start and end apart: 12 -> 0, of which waited for: 2 -> 0; matrix products, arithmetic and copies ran while one was open for 38% -> 0% of each run, Pallas kernels for 0% -> 0%
where the time goes in v1:
time: 35.2 us; the launch traced here: 34.9 us
  Pallas kernels  28.3 us (80%)
  local copies, waits for them, and re-layouts  5.96 us (17%)
  between operations  0.65 us (2%)
    pallas_call x1, Pallas kernels, on_device(): pl.pallas_call(functools.partial(kernel, n_col, n_tile, 4 * rows * cols *...  28.3 us
    unnamed x12, local copies, waits for them, and re-layouts  5.96 us

profile of v1, /device:TPU:0, one launch (start us, length us, event | category | flops | bytes accessed | tf_op | source)
XLA Modules:
  0.0 34.9 jit_solution(14316247962592219144)
XLA Ops:
  0.6 0.0 copy-start
  0.6 1.0 %copy-done = f32[8,4,8,512]{3,2,1,0:T(8,128)S(1)} copy-done((f32[8,4,8,512]{3,2,1,0:T(8,128)S(1)}, f32[8,4,8,512]{3,2,1,0:T(8,128)}, u32[]{:S(2)}) %copy-start) | copy-done | bytes 524312
  1.7 0.0 copy-start.1
  1.7 0.9 %copy-done.1 = s32[4,2,8,512]{3,2,1,0:T(8,128)S(1)} copy-done((s32[4,2,8,512]{3,2,1,0:T(8,128)S(1)}, s32[4,2,8,512]{3,2,1,0:T(8,128)}, u32[]{:S(2)}) %copy-start.1) | copy-done | bytes 131096
  2.6 0.0 copy-start.2
  2.6 0.9 %copy-done.2 = f32[4,2,8,512]{3,2,1,0:T(8,128)S(1)} copy-done((f32[4,2,8,512]{3,2,1,0:T(8,128)S(1)}, f32[4,2,8,512]{3,2,1,0:T(8,128)}, u32[]{:S(2)}) %copy-start.2) | copy-done | bytes 131096
  3.5 0.0 copy-start.3
  3.5 0.9 %copy-done.3 = f32[3,2,8,512]{3,2,1,0:T(8,128)S(1)} copy-done((f32[3,2,8,512]{3,2,1,0:T(8,128)S(1)}, f32[3,2,8,512]{3,2,1,0:T(8,128)}, u32[]{:S(2)}) %copy-start.3) | copy-done | bytes 98328
  4.4 0.0 copy-start.4
  4.4 0.8 %copy-done.4 = f32[4,8,512]{2,1,0:T(8,128)S(1)} copy-done((f32[4,8,512]{2,1,0:T(8,128)S(1)}, f32[4,8,512]{2,1,0:T(8,128)}, u32[]{:S(2)}) %copy-start.4) | copy-done | bytes 65560
  5.2 28.3 %shard_map.68 = (f32[8,4,8,512]{3,2,1,0:T(8,128)S(1)}, f32[7,8]{1,0:T(8,128)S(1)}) custom-call(f32[8,4,8,512]{3,2,1,0:T(8,128)S(1)} %copy-done, f32[4,8,512]{2,1,0:T(8,128)S(1)} %copy-done.4, f32[6,8,512]{2,1,0:T(8,128)S(1)} %bitcast.5, s32[8,8,512]{2,1,0:T(8,128)S(1)} %bitcast.3, f32[8,8,512]{2,1,0:T(8,128)S(1)} %bitcast.4), custom_call_target="tpu_custom_call" | custom-call | tf_op jit(solution)/shard_map/pallas_call | solution.py:303
  33.5 0.8 %copy.9 = f32[8,4,8,512]{3,2,1,0:T(8,128)} copy(f32[8,4,8,512]{3,2,1,0:T(8,128)S(1)} %get-tuple-element.4) | data formatting | bytes 1048576
  34.3 0.6 %copy.10 = f32[7,8]{1,0:T(8,128)} copy(f32[7,8]{1,0:T(8,128)S(1)} %get-tuple-element.5) | data formatting | bytes 448
Async XLA Ops:
  0.6 1.0 %copy-start = (f32[8,4,8,512]{3,2,1,0:T(8,128)S(1)}, f32[8,4,8,512]{3,2,1,0:T(8,128)}, u32[]{:S(2)}) copy-start(f32[8,4,8,512]{3,2,1,0:T(8,128)} %v_ref.1) | copy-start | bytes 1572868
  1.7 0.9 %copy-start.1 = (s32[4,2,8,512]{3,2,1,0:T(8,128)S(1)}, s32[4,2,8,512]{3,2,1,0:T(8,128)}, u32[]{:S(2)}) copy-start(s32[4,2,8,512]{3,2,1,0:T(8,128)} %param.8) | copy-start | bytes 393220
  2.6 0.9 %copy-start.2 = (f32[4,2,8,512]{3,2,1,0:T(8,128)S(1)}, f32[4,2,8,512]{3,2,1,0:T(8,128)}, u32[]{:S(2)}) copy-start(f32[4,2,8,512]{3,2,1,0:T(8,128)} %param.9) | copy-start | bytes 393220
  3.5 0.9 %copy-start.3 = (f32[3,2,8,512]{3,2,1,0:T(8,128)S(1)}, f32[3,2,8,512]{3,2,1,0:T(8,128)}, u32[]{:S(2)}) copy-start(f32[3,2,8,512]{3,2,1,0:T(8,128)} %param.7) | copy-start | bytes 294916
  4.4 0.8 %copy-start.4 = (f32[4,8,512]{2,1,0:T(8,128)S(1)}, f32[4,8,512]{2,1,0:T(8,128)}, u32[]{:S(2)}) copy-start(f32[4,8,512]{2,1,0:T(8,128)} %onsite_ref.1) | copy-start | bytes 196612

commit v2 on v1

--- a/solution.py
+++ b/solution.py
@@ -7,7 +7,7 @@
 from jax.experimental.pallas import tpu as pltpu
 from jax.sharding import PartitionSpec as P
 
-RIM = 3
+RIM = 2
 LANES = 128
 CODES = 18
 MESH = pl.DeviceIdType.MESH
@@ -17,8 +17,9 @@
 
 def kernel(
     n_col, n_tile, orbitals,
-    v_ref, onsite_ref, intra_ref, index_ref, hop_ref,
+    v_hbm, onsite_hbm, intra_hbm, index_hbm, hop_hbm,
     out_ref, mom_ref,
+    v_ref, onsite_ref, intra_ref, index_ref, hop_ref, load_sem,
     area, terms, moved, weights, weights_t, bond_t, packs, halo, sums, part, col_buf, col_sum, tile_buf,
     row_send, row_recv, pack_send, pack_recv, col_send, col_recv, tile_send, tile_recv,
 ):
@@ -37,6 +38,21 @@
     def tile_at(step):
         return lax.rem(my_tile + step + n_tile, n_tile)
 
+    loads = [
+        pltpu.make_async_copy(src, dst, load_sem.at[n])
+        for n, (src, dst) in enumerate(
+            (
+                (v_hbm, v_ref),
+                (hop_hbm, hop_ref),
+                (index_hbm, index_ref),
+                (onsite_hbm, onsite_ref),
+                (intra_hbm, intra_ref),
+            )
+        )
+    ]
+    for load in loads:
+        load.start()
+
     barrier = pltpu.get_barrier_semaphore()
     greeted = [(col_at(c), tile_at(t)) for c in (-1, 1) for t in (-1, 1)]
     greeted += [(col_at(c), my_tile) for c in range(1, n_col)]
@@ -49,6 +65,8 @@
 
     lax.fori_loop(1, n_tile, greet, 0)
 
+    for load in loads:
+        load.wait()
     own = slice(RIM, RIM + rows)
     for o in range(4):
         area[o, own, :, 0:cols] = jnp.swapaxes(v_ref[:, o], 0, 1)
@@ -63,18 +81,30 @@
 
     pl.semaphore_wait(barrier, len(greeted) + n_tile - 1)
 
-    row_copies = []
-    for way, (src, dst, step) in enumerate(((rows, 0, 1), (RIM, RIM + rows, -1))):
+    rim_copies = []
+
+    def send_rim(layer, way, src, dst):
         copy = pltpu.make_async_remote_copy(
-            src_ref=area.at[:, src : src + RIM, :, 0:cols],
-            dst_ref=area.at[:, dst : dst + RIM, :, 0:cols],
-            send_sem=row_send.at[way],
-            recv_sem=row_recv.at[way],
-            device_id=(my_col, tile_at(step)),
+            src_ref=src,
+            dst_ref=dst,
+            send_sem=row_send.at[layer, way],
+            recv_sem=row_recv.at[layer, way],
+            device_id=(my_col, tile_at(1 - 2 * way)),
             device_id_type=MESH,
         )
         copy.start()
-        row_copies.append(copy)
+        rim_copies.append(copy)
+
+    low, high = RIM, RIM + rows
+    for layer in range(2):
+        for way in range(2):
+            src, dst = ((high - 1 - layer, low - 1 - layer), (low + layer, high + layer))[way]
+            groups = 8 if layer == 0 else 6 + way
+            send_rim(
+                layer, way,
+                area.at[0:groups, src : src + 1, :, 0:cols],
+                area.at[0:groups, dst : dst + 1, :, 0:cols],
+            )
 
     def pack(r, carry):
         out = list(carry)
@@ -112,15 +142,16 @@
     def rolls(x):
         return pltpu.roll(x, 1, 1), pltpu.roll(x, ring - 1, 1)
 
-    def prepare(r, theirs, dt):
-        for g in range(8):
+    def prepare(r, theirs, dt, groups=8):
+        for g in range(groups):
             i = (g % 4) * rows + theirs
             from_right = pltpu.roll(halo[1 + dt, g // 4], lax.rem(LANES - 4 * i, LANES), 1)
             from_left = pltpu.roll(halo[4 + dt, g // 4], LANES - 4 - 4 * i, 1)
             area[g, r, :, cols:ring] = jnp.where(lane < LANES // 2, from_right, from_left)
         for o in range(4):
             moved[0, 0, o, r], moved[0, 1, o, r] = rolls(area[o, r])
-        bond_t[r] = rolls(area[BOND2, r])[1]
+        if groups == 8:
+            bond_t[r] = rolls(area[BOND2, r])[1]
         for s in range(2):
             for b in range(blocks + 1):
                 at = slice(b * LANES, (b + 1) * LANES)
@@ -212,21 +243,28 @@
 
     for n in (0, 3):
         pack_copies[n].wait_recv()
-    loop(RIM, RIM + rows, lambda r: prepare(r, r - RIM, 0))
+    loop(low, high, lambda r: prepare(r, r - low, 0))
     for k in range(3):
-        loop(RIM + 1 + k, RIM + rows - 1 - k, functools.partial(advance, k))
+        loop(low + 1 + k, high - 1 - k, functools.partial(advance, k))
+        if k == 1:
+            send_rim(2, 0, terms.at[0, :, high - 2 : high - 1], terms.at[0, :, 0:1])
+            send_rim(2, 1, terms.at[0, :, low + 1 : low + 2], terms.at[0, :, high + 1 : high + 2])
 
     for n in (1, 2, 4, 5):
         pack_copies[n].wait_recv()
-    for copy in row_copies:
-        copy.wait_recv()
-    loop(0, RIM, lambda r: prepare(r, rows - RIM + r, -1))
-    loop(0, RIM, lambda r: prepare(RIM + rows + r, r, 1))
-    for k in range(3):
-        def outer(i, k=k):
-            advance(k, k + 1 + i + (i // 3) * (rows - 2 * k - 2))
-
-        loop(0, 6, outer)
+    for layer in range(3):
+        for way in range(2):
+            rim_copies[2 * layer + way].wait_recv()
+        if layer < 2:
+            prepare(low - 1 - layer, rows - 1 - layer, -1, 8 if layer == 0 else 6)
+            prepare(high + layer, layer, 1, 8 if layer == 0 else 7)
+        else:
+            for r in (0, high + 1):
+                for o in range(4):
+                    moved[1, 0, o, r], moved[1, 1, o, r] = rolls(terms[0, o, r])
+        for k in range(1 if layer == 2 else 0, 3):
+            top, bottom = low - layer + k, high - 1 + layer - k
+            loop(0, 2, lambda i, k=k: advance(k, top + i * (bottom - top)))
 
     row = jnp.zeros((8, LANES), jnp.float32)
     for n in range(7):
@@ -278,7 +316,7 @@
         )
 
     loop(1, n_tile, lambda i: tile_copy(i, my_tile).start())
-    for copy in row_copies + pack_copies + col_copies:
+    for copy in rim_copies + pack_copies + col_copies:
         copy.wait_send()
     loop(1, n_tile, lambda i: tile_copy(i, lax.rem(my_tile + n_tile - i, n_tile)).wait_recv())
     loop(1, n_tile, lambda i: tile_copy(i, my_tile).wait_send())
@@ -306,9 +344,15 @@
             jax.ShapeDtypeStruct(vectors.shape, f32),
             jax.ShapeDtypeStruct((7, count), f32),
         ),
-        in_specs=[vmem] * 5,
+        in_specs=[pl.BlockSpec(memory_space=pl.ANY)] * 5,
         out_specs=(vmem, vmem),
         scratch_shapes=[
+            pltpu.VMEM(vectors.shape, f32),
+            pltpu.VMEM(onsite.shape, f32),
+            pltpu.VMEM((6, rows, cols), f32),
+            pltpu.VMEM((2 * slots, rows, cols), jnp.int32),
+            pltpu.VMEM((2 * slots, rows, cols), f32),
+            dma((5,)),
             pltpu.VMEM((8, tall, 8, ring), f32),
             pltpu.VMEM((3, 4, tall, 8, ring), f32),
             pltpu.VMEM((3, 2, 4, tall, 8, ring), f32),
@@ -322,11 +366,11 @@
             pltpu.VMEM((n_col, 1, LANES), f32),
             pltpu.VMEM((1, LANES), f32),
             pltpu.VMEM((n_tile, 1, LANES), f32),
-            dma((2,)), dma((2,)), dma((6,)), dma((6,)),
+            dma((3, 2)), dma((3, 2)), dma((6,)), dma((6,)),
             dma((n_col,)), dma((n_col,)), dma((n_tile,)), dma((n_tile,)),
         ],
         compiler_params=pltpu.CompilerParams(
-            collective_id=0, has_side_effects=True, vmem_limit_bytes=48 << 20
+            collective_id=0, has_side_effects=True, vmem_limit_bytes=60 << 20
         ),
     )(
         vectors,

time: 35.2 us -> 29.3 us (0.83)
  local copies, waits for them, and re-layouts: 5.96 us -> 2.47 us
  Pallas kernels: 28.3 us -> 26 us
    unnamed x12 -> x4, local copies, waits for them, and re-layouts: 5.96 us -> 2.47 us
    pallas_call x1, Pallas kernels: 28.3 us -> 26 us  [on_device(): pl.pallas_call(functools.partial(kernel, n_col, n_tile, 4 * rows * cols *...]
where the time goes in v2:
time: 29.3 us; the launch traced here: 29.1 us
  Pallas kernels  26 us (89%)
  local copies, waits for them, and re-layouts  2.47 us (8%)
  between operations  0.65 us (2%)
    pallas_call x1, Pallas kernels, on_device(): pl.pallas_call(functools.partial(kernel, n_col, n_tile, 4 * rows * cols *...  26 us
    unnamed x4, local copies, waits for them, and re-layouts  2.47 us

profile of v2, /device:TPU:0, one launch (start us, length us, event | category | flops | bytes accessed | tf_op | source)
XLA Modules:
  0.0 29.1 jit_solution(8825157147130522093)
XLA Ops:
  0.6 26.0 %shard_map.68 = (f32[8,4,8,512]{3,2,1,0:T(8,128)}, f32[7,8]{1,0:T(8,128)}) custom-call(f32[8,4,8,512]{3,2,1,0:T(8,128)} %v_hbm.1, f32[4,8,512]{2,1,0:T(8,128)} %onsite_hbm.1, f32[6,8,512]{2,1,0:T(8,128)} %bitcast.5, s32[8,8,512]{2,1,0:T(8,128)} %bitcast.3, f32[8,8,512]{2,1,0:T(8,128)} %bitcast.4), custom_call_target="tpu_custom_call" | custom-call | tf_op jit(solution)/shard_map/pallas_call | solution.py:341
  26.7 0.0 copy-start
  26.7 1.9 %copy.9 = f32[8,4,8,512]{3,2,1,0:T(8,128)} copy(f32[8,4,8,512]{3,2,1,0:T(8,128)} %get-tuple-element.4) | data formatting | bytes 1048576
  28.5 0.0 copy-done
  28.5 0.6 %copy.10 = f32[7,8]{1,0:T(8,128)} copy(f32[7,8]{1,0:T(8,128)S(1)} %copy-done) | data formatting | bytes 448
Async XLA Ops:
  26.7 1.9 %copy-start = (f32[7,8]{1,0:T(8,128)S(1)}, f32[7,8]{1,0:T(8,128)}, u32[]{:S(2)}) copy-start(f32[7,8]{1,0:T(8,128)} %get-tuple-element.5) | copy-start | bytes 676

commit v3 on v2

--- a/solution.py
+++ b/solution.py
@@ -20,8 +20,8 @@
     v_hbm, onsite_hbm, intra_hbm, index_hbm, hop_hbm,
     out_ref, mom_ref,
     v_ref, onsite_ref, intra_ref, index_ref, hop_ref, load_sem,
-    area, terms, moved, weights, weights_t, bond_t, packs, halo, sums, part, col_buf, col_sum, tile_buf,
-    row_send, row_recv, pack_send, pack_recv, col_send, col_recv, tile_send, tile_recv,
+    area, terms, moved, weights, weights_t, bond_t, packs, halo, sums, part, all_parts,
+    row_send, row_recv, pack_send, pack_recv, part_send, part_recv,
 ):
     rows = v_ref.shape[2]
     cols = v_ref.shape[3]
@@ -54,16 +54,18 @@
         load.start()
 
     barrier = pltpu.get_barrier_semaphore()
-    greeted = [(col_at(c), tile_at(t)) for c in (-1, 1) for t in (-1, 1)]
-    greeted += [(col_at(c), my_tile) for c in range(1, n_col)]
-    for c, t in greeted:
-        pl.semaphore_signal(barrier, inc=1, device_id=(c, t), device_id_type=MESH)
+    devices = n_col * n_tile
+    me = my_col * n_tile + my_tile
+
+    def device(step):
+        at = lax.rem(me + step, devices)
+        return (lax.div(at, n_tile), lax.rem(at, n_tile))
 
     def greet(i, carry):
-        pl.semaphore_signal(barrier, inc=1, device_id=(my_col, lax.rem(my_tile + i, n_tile)), device_id_type=MESH)
+        pl.semaphore_signal(barrier, inc=1, device_id=device(i), device_id_type=MESH)
         return carry
 
-    lax.fori_loop(1, n_tile, greet, 0)
+    lax.fori_loop(1, devices, greet, 0)
 
     for load in loads:
         load.wait()
@@ -79,7 +81,65 @@
         jnp.concatenate([intra_ref[4:6], jnp.zeros((6, rows, cols), jnp.float32)], axis=0), 0, 1
     )
 
-    pl.semaphore_wait(barrier, len(greeted) + n_tile - 1)
+    def pack(r, carry):
+        out = list(carry)
+        for g in range(8):
+            i = (g % 4) * rows + r
+            hit = lane // 4 == i
+            left = pltpu.roll(area[g, RIM + r, :, 0:LANES], 4 * i, 1)
+            right = pltpu.roll(area[g, RIM + r, :, cols - LANES : cols], lax.rem(4 * i + 4, LANES), 1)
+            out[g // 4] = jnp.where(hit, left, out[g // 4])
+            out[2 + g // 4] = jnp.where(hit, right, out[2 + g // 4])
+        return tuple(out)
+
+    zero = jnp.zeros((8, LANES), jnp.float32)
+    packed = lax.fori_loop(0, rows, pack, (zero,) * 4)
+    for n in range(4):
+        packs[n // 2, n % 2] = packed[n]
+
+    def weigh(r, at_blocks):
+        for s in range(2):
+            for b in at_blocks:
+                at = slice(b * LANES, (b + 1) * LANES)
+                total = [zero] * 3
+                for k in range(4):
+                    f = 2 * k + s
+                    code = jnp.broadcast_to(area[CODE, r, f : f + 1, at], (8, LANES)).astype(jnp.int32)
+                    hop = jnp.broadcast_to(area[HOP, r, f : f + 1, at], (8, LANES))
+                    for g in range(3):
+                        total[g] = total[g] + jnp.where(code == sub + 8 * g, hop, 0.0)
+                for g in range(3):
+                    weights[r, s, 8 * g : 8 * g + 8, at] = total[g]
+
+    def loop(low, high, body):
+        def step(i, carry):
+            body(i)
+            return carry
+
+        lax.fori_loop(low, high, step, 0)
+
+    low, high = RIM, RIM + rows
+    loop(low, high, lambda r: weigh(r, range(blocks)))
+    for n in range(7):
+        sums[n] = zero
+
+    pl.semaphore_wait(barrier, devices - 1)
+
+    pack_copies = []
+    for side, step in ((0, -1), (1, 1)):
+        for dt in (0, -1, 1):
+            slot = side * 3 + 1 - dt
+            copy = pltpu.make_async_remote_copy(
+                src_ref=packs.at[side],
+                dst_ref=halo.at[slot],
+                send_sem=pack_send.at[slot],
+                recv_sem=pack_recv.at[slot],
+                device_id=(col_at(step), tile_at(dt)),
+                device_id_type=MESH,
+            )
+            copy.start()
+            pack_copies.append(copy)
+
 
     rim_copies = []
 
@@ -95,7 +155,6 @@
         copy.start()
         rim_copies.append(copy)
 
-    low, high = RIM, RIM + rows
     for layer in range(2):
         for way in range(2):
             src, dst = ((high - 1 - layer, low - 1 - layer), (low + layer, high + layer))[way]
@@ -105,37 +164,6 @@
                 area.at[0:groups, src : src + 1, :, 0:cols],
                 area.at[0:groups, dst : dst + 1, :, 0:cols],
             )
-
-    def pack(r, carry):
-        out = list(carry)
-        for g in range(8):
-            i = (g % 4) * rows + r
-            hit = lane // 4 == i
-            left = pltpu.roll(area[g, RIM + r, :, 0:LANES], 4 * i, 1)
-            right = pltpu.roll(area[g, RIM + r, :, cols - LANES : cols], lax.rem(4 * i + 4, LANES), 1)
-            out[g // 4] = jnp.where(hit, left, out[g // 4])
-            out[2 + g // 4] = jnp.where(hit, right, out[2 + g // 4])
-        return tuple(out)
-
-    zero = jnp.zeros((8, LANES), jnp.float32)
-    packed = lax.fori_loop(0, rows, pack, (zero,) * 4)
-    for n in range(4):
-        packs[n // 2, n % 2] = packed[n]
-
-    pack_copies = []
-    for side, step in ((0, -1), (1, 1)):
-        for dt in (0, -1, 1):
-            slot = side * 3 + 1 - dt
-            copy = pltpu.make_async_remote_copy(
-                src_ref=packs.at[side],
-                dst_ref=halo.at[slot],
-                send_sem=pack_send.at[slot],
-                recv_sem=pack_recv.at[slot],
-                device_id=(col_at(step), tile_at(dt)),
-                device_id_type=MESH,
-            )
-            copy.start()
-            pack_copies.append(copy)
 
     wide = lax.broadcasted_iota(jnp.int32, (8, ring), 0)
 
@@ -152,18 +180,8 @@
             moved[0, 0, o, r], moved[0, 1, o, r] = rolls(area[o, r])
         if groups == 8:
             bond_t[r] = rolls(area[BOND2, r])[1]
+        weigh(r, (blocks,) if dt == 0 else range(blocks + 1))
         for s in range(2):
-            for b in range(blocks + 1):
-                at = slice(b * LANES, (b + 1) * LANES)
-                total = [zero] * 3
-                for k in range(4):
-                    f = 2 * k + s
-                    code = jnp.broadcast_to(area[CODE, r, f : f + 1, at], (8, LANES)).astype(jnp.int32)
-                    hop = jnp.broadcast_to(area[HOP, r, f : f + 1, at], (8, LANES))
-                    for g in range(3):
-                        total[g] = total[g] + jnp.where(code == sub + 8 * g, hop, 0.0)
-                for g in range(3):
-                    weights[r, s, 8 * g : 8 * g + 8, at] = total[g]
             for g in range(3):
                 x = weights[r, s, 8 * g : 8 * g + 8, :]
                 back, ahead = rolls(x)
@@ -231,16 +249,6 @@
             for o in range(4):
                 moved[k + 1, 0, o, r], moved[k + 1, 1, o, r] = rolls(terms[k, o, r])
 
-    def loop(low, high, body):
-        def step(i, carry):
-            body(i)
-            return carry
-
-        lax.fori_loop(low, high, step, 0)
-
-    for n in range(7):
-        sums[n] = zero
-
     for n in (0, 3):
         pack_copies[n].wait_recv()
     loop(low, high, lambda r: prepare(r, r - low, 0))
@@ -271,56 +279,29 @@
         total = jnp.sum(sums[n], axis=1, keepdims=True)
         row = jnp.where(lane == sub + 8 * n, jnp.broadcast_to(total, (8, LANES)), row)
     part[...] = jnp.sum(row, axis=0, keepdims=True)
-    col_buf[my_col] = part[...]
-    col_copies = []
-    for step in range(1, n_col):
-        copy = pltpu.make_async_remote_copy(
+    all_parts[me] = part[...]
+
+    def part_copy(step, slot):
+        return pltpu.make_async_remote_copy(
             src_ref=part,
-            dst_ref=col_buf.at[my_col],
-            send_sem=col_send.at[step],
-            recv_sem=col_recv.at[step],
-            device_id=(col_at(step), my_tile),
+            dst_ref=all_parts.at[slot],
+            send_sem=part_send.at[step],
+            recv_sem=part_recv.at[step],
+            device_id=device(step),
             device_id_type=MESH,
         )
-        copy.start()
-        col_copies.append(copy)
+
+    loop(1, devices, lambda i: part_copy(i, me).start())
     for o in range(4):
         out_ref[:, o] = jnp.swapaxes(terms[2, o, own, :, 0:cols], 0, 1)
 
-    def col_done(step):
-        return pltpu.make_async_remote_copy(
-            src_ref=part,
-            dst_ref=col_buf.at[col_at(-step)],
-            send_sem=col_send.at[step],
-            recv_sem=col_recv.at[step],
-            device_id=(col_at(step), my_tile),
-            device_id_type=MESH,
-        )
-
-    for step in range(1, n_col):
-        col_done(step).wait_recv()
-    total = col_buf[0]
-    for n in range(1, n_col):
-        total = total + col_buf[n]
-    col_sum[...] = total
-    tile_buf[my_tile] = col_sum[...]
-
-    def tile_copy(step, slot):
-        return pltpu.make_async_remote_copy(
-            src_ref=col_sum,
-            dst_ref=tile_buf.at[slot],
-            send_sem=tile_send.at[step],
-            recv_sem=tile_recv.at[step],
-            device_id=(my_col, lax.rem(my_tile + step, n_tile)),
-            device_id_type=MESH,
-        )
-
-    loop(1, n_tile, lambda i: tile_copy(i, my_tile).start())
-    for copy in rim_copies + pack_copies + col_copies:
+    for copy in rim_copies + pack_copies:
         copy.wait_send()
-    loop(1, n_tile, lambda i: tile_copy(i, lax.rem(my_tile + n_tile - i, n_tile)).wait_recv())
-    loop(1, n_tile, lambda i: tile_copy(i, my_tile).wait_send())
-    total = lax.fori_loop(1, n_tile, lambda i, t: t + tile_buf[i], tile_buf[0])
+    loop(1, devices, lambda i: part_copy(i, lax.rem(me + devices - i, devices)).wait_recv())
+    loop(1, devices, lambda i: part_copy(i, me).wait_send())
+    total = all_parts[0]
+    for n in range(1, devices):
+        total = total + all_parts[n]
     total = jnp.broadcast_to(total / orbitals, (8, LANES))
     scaled = [pltpu.roll(total, (LANES - 8 * n) % LANES, 1)[0:1, 0:8] for n in range(7)]
     mom_ref[0:1, :] = scaled[0]
@@ -344,7 +325,7 @@
             jax.ShapeDtypeStruct(vectors.shape, f32),
             jax.ShapeDtypeStruct((7, count), f32),
         ),
-        in_specs=[pl.BlockSpec(memory_space=pl.ANY)] * 5,
+        in_specs=[pl.BlockSpec(memory_space=pltpu.HBM)] * 5,
         out_specs=(vmem, vmem),
         scratch_shapes=[
             pltpu.VMEM(vectors.shape, f32),
@@ -363,21 +344,24 @@
             pltpu.VMEM((6, 2, 8, LANES), f32),
             pltpu.VMEM((7, 8, LANES), f32),
             pltpu.VMEM((1, LANES), f32),
-            pltpu.VMEM((n_col, 1, LANES), f32),
-            pltpu.VMEM((1, LANES), f32),
-            pltpu.VMEM((n_tile, 1, LANES), f32),
+            pltpu.VMEM((n_col * n_tile, 1, LANES), f32),
             dma((3, 2)), dma((3, 2)), dma((6,)), dma((6,)),
-            dma((n_col,)), dma((n_col,)), dma((n_tile,)), dma((n_tile,)),
+            dma((n_col * n_tile,)), dma((n_col * n_tile,)),
         ],
         compiler_params=pltpu.CompilerParams(
-            collective_id=0, has_side_effects=True, vmem_limit_bytes=60 << 20
+            collective_id=0, has_side_effects=True, vmem_limit_bytes=32 << 20
         ),
     )(
-        vectors,
-        onsite,
-        intra_hop.reshape(6, rows, cols),
-        inter_index.reshape(2 * slots, rows, cols),
-        inter_hop.reshape(2 * slots, rows, cols),
+        *(
+            pltpu.with_memory_space_constraint(x, pltpu.HBM)
+            for x in (
+                vectors,
+                onsite,
+                intra_hop.reshape(6, rows, cols),
+                inter_index.reshape(2 * slots, rows, cols),
+                inter_hop.reshape(2 * slots, rows, cols),
+            )
+        )
     )
 
 

time: 29.3 us -> 26.6 us (0.908)
  Pallas kernels: 26 us -> 24.4 us
  local copies, waits for them, and re-layouts: 2.47 us -> 1.39 us
    pallas_call x1, Pallas kernels: 26 us -> 24.4 us  [on_device(): pl.pallas_call(functools.partial(kernel, n_col, n_tile, 4 * rows * cols *...]
    unnamed x4 -> x2, local copies, waits for them, and re-layouts: 2.47 us -> 1.39 us
where the time goes in v3:
time: 26.6 us; the launch traced here: 26.4 us
  Pallas kernels  24.4 us (92%)
  local copies, waits for them, and re-layouts  1.39 us (5%)
  between operations  0.64 us (2%)
    pallas_call x1, Pallas kernels, on_device(): pl.pallas_call(functools.partial(kernel, n_col, n_tile, 4 * rows * cols *...  24.4 us
    unnamed x2, local copies, waits for them, and re-layouts  1.39 us

profile of v3, /device:TPU:0, one launch (start us, length us, event | category | flops | bytes accessed | tf_op | source)
XLA Modules:
  0.0 26.4 jit_solution(6911562018829020214)
XLA Ops:
  0.6 24.4 %shard_map.68 = (f32[8,4,8,512]{3,2,1,0:T(8,128)S(1)}, f32[7,8]{1,0:T(8,128)S(1)}) custom-call(f32[8,4,8,512]{3,2,1,0:T(8,128)} %v_hbm.1, f32[4,8,512]{2,1,0:T(8,128)} %onsite_hbm.1, f32[6,8,512]{2,1,0:T(8,128)} %bitcast.5, s32[8,8,512]{2,1,0:T(8,128)} %bitcast.3, f32[8,8,512]{2,1,0:T(8,128)} %bitcast.4), custom_call_target="tpu_custom_call" | custom-call | tf_op jit(solution)/shard_map/pallas_call | solution.py:322
  25.0 0.8 %copy.9 = f32[8,4,8,512]{3,2,1,0:T(8,128)} copy(f32[8,4,8,512]{3,2,1,0:T(8,128)S(1)} %get-tuple-element.4) | data formatting | bytes 1048576
  25.8 0.6 %copy.10 = f32[7,8]{1,0:T(8,128)} copy(f32[7,8]{1,0:T(8,128)S(1)} %get-tuple-element.5) | data formatting | bytes 448

commit v4 on v3

--- a/solution.py
+++ b/solution.py
@@ -310,6 +310,17 @@
         mom_ref[n : n + 1, :] = 2.0 * scaled[n] - scaled[n % 2]
 
 
+def emit(last_ref, rows_ref, out_ref, mom_ref, sem):
+    copies = [
+        pltpu.make_async_copy(last_ref, out_ref, sem.at[0]),
+        pltpu.make_async_copy(rows_ref, mom_ref, sem.at[1]),
+    ]
+    for copy in copies:
+        copy.start()
+    for copy in copies:
+        copy.wait()
+
+
 def on_device(n_col, n_tile, vectors, onsite, intra_hop, inter_index, inter_hop):
     count, _, rows, cols = vectors.shape
     slots = inter_index.shape[0]
@@ -319,7 +330,7 @@
     f32 = jnp.float32
     vmem = pl.BlockSpec(memory_space=pltpu.VMEM)
     dma = pltpu.SemaphoreType.DMA
-    return pl.pallas_call(
+    results = pl.pallas_call(
         functools.partial(kernel, n_col, n_tile, 4 * rows * cols * n_col * n_tile),
         out_shape=(
             jax.ShapeDtypeStruct(vectors.shape, f32),
@@ -363,6 +374,18 @@
             )
         )
     )
+    kept = pl.BlockSpec(memory_space=pl.ANY)
+    return pl.pallas_call(
+        emit,
+        out_shape=(
+            jax.ShapeDtypeStruct(vectors.shape, f32),
+            jax.ShapeDtypeStruct((7, count), f32),
+        ),
+        in_specs=[kept] * 2,
+        out_specs=(kept, kept),
+        scratch_shapes=[dma((2,))],
+        compiler_params=pltpu.CompilerParams(vmem_limit_bytes=1 << 20),
+    )(*results)
 
 
 def solution(mesh):

time: 26.6 us -> 26 us (0.977)
  local copies, waits for them, and re-layouts: 1.39 us -> 0 us
  Pallas kernels: 24.4 us -> 25.2 us
    unnamed x2 -> x0, local copies, waits for them, and re-layouts: 1.39 us -> none
    pallas_call x0 -> x1, Pallas kernels: none -> 0.81 us  [on_device(): pl.pallas_call(emit, out_shape=(jax.ShapeDtypeStruct(vectors.shape, f32),...]
where the time goes in v4:
time: 26 us; the launch traced here: 25.8 us
  Pallas kernels  25.2 us (97%)
  between operations  0.64 us (2%)
    pallas_call x1, Pallas kernels, on_device(): pl.pallas_call(functools.partial(kernel, n_col, n_tile, 4 * rows * cols *...  24.4 us
    pallas_call x1, Pallas kernels, on_device(): pl.pallas_call(emit, out_shape=(jax.ShapeDtypeStruct(vectors.shape, f32),...  0.81 us

profile of v4, /device:TPU:0, one launch (start us, length us, event | category | flops | bytes accessed | tf_op | source)
XLA Modules:
  0.0 25.8 jit_solution(12244800505730236059)
XLA Ops:
  0.6 24.4 %shard_map.68 = (f32[8,4,8,512]{3,2,1,0:T(8,128)S(1)}, f32[7,8]{1,0:T(8,128)S(1)}) custom-call(f32[8,4,8,512]{3,2,1,0:T(8,128)} %v_hbm.1, f32[4,8,512]{2,1,0:T(8,128)} %onsite_hbm.1, f32[6,8,512]{2,1,0:T(8,128)} %bitcast.5, s32[8,8,512]{2,1,0:T(8,128)} %bitcast.3, f32[8,8,512]{2,1,0:T(8,128)} %bitcast.4), custom_call_target="tpu_custom_call" | custom-call | tf_op jit(solution)/shard_map/pallas_call | solution.py:333
  25.0 0.8 %shard_map.69 = (f32[8,4,8,512]{3,2,1,0:T(8,128)}, f32[7,8]{1,0:T(8,128)}) custom-call(f32[8,4,8,512]{3,2,1,0:T(8,128)S(1)} %get-tuple-element.4.last_ref, f32[7,8]{1,0:T(8,128)S(1)} %get-tuple-element.5.rows_ref), custom_call_target="tpu_custom_call" | custom-call | tf_op jit(solution)/shard_map/pallas_call | solution.py:378
